TPU v7x, 32 devices: a whole 2x2x4 slice. The times are simulated.
32 devices in a mesh: seq: 8 (over y, x, core), tensor: 4 (over z).
Axes of the slice: x: 2, y: 2, z: 4, core: 2. Of those that a mesh axis runs over, the one named last changes fastest.
Arguments:
- queries: bfloat16 [1024, 4096], P(('seq', 'tensor')), may hold values from -5 to 5
- keys: bfloat16 [1024, 1024], P(('seq', 'tensor')), may hold values from -5 to 5
- values: bfloat16 [1024, 1024], P(('seq', 'tensor')), may hold values from -5 to 5
- mamba_x: bfloat16 [1024, 8192], P(('seq', 'tensor')), may hold values from -5 to 5
- mamba_b: bfloat16 [1024, 1024], P(('seq', 'tensor')), may hold values from -5 to 5
- mamba_c: bfloat16 [1024, 1024], P(('seq', 'tensor')), may hold values from -5 to 5
- mamba_dt: bfloat16 [1024, 128], P(('seq', 'tensor')), may hold values from -4 to 4
- conv_x: bfloat16 [4, 8192], P(None, 'tensor'), may hold values from -3 to 3
- conv_b: bfloat16 [4, 1024], P(None, 'tensor'), may hold values from -3 to 3
- conv_c: bfloat16 [4, 1024], P(None, 'tensor'), may hold values from -3 to 3
- dt_bias: float32 [128], P('tensor'), may hold values from -1 to 1
- decay_rate: float32 [128], P('tensor'), may hold values from 0.0001 to 0.05
- skip_gain: float32 [128], P('tensor'), may hold values from 0.5 to 1.5
- norm_gain: float32 [8192], P('tensor'), may hold values from 0.5 to 1.5
- windows: int32 [32], replicated, may hold values from 160 to 640, as said below
- doc_lengths: int32 [3], replicated, may hold values from 1 to 768, 1024 in all
Outputs:
- attn_out: bfloat16 [1024, 4096], P('seq', 'tensor')
- mamba_out: bfloat16 [1024, 8192], P('seq', 'tensor')
- attn_checksum: float32 [4096], P('tensor')
- mamba_checksum: float32 [8192], P('tensor')
Inputs may be any that keep to these rules, and one draw needn't show every extreme that they name: `windows`: one of the 32 query heads has a window of exactly 640 tokens. `doc_lengths`: 3 lengths summing to 1024; the longest is exactly three quarters of 1024.
All inputs are finite; a program needn't handle non-finite values.
Results may differ from a plain program's by a relative error of at most 0.007.
Values may be sent and summed in bfloat16 or wider, within the bound.
No kernel may reach another device: no remote copies, remote signals or barrier semaphores. Data moves between devices by JAX's collectives and lax.ppermute only.
A program may use at most 192 MiB of HBM per device.

v0:
```python
import math

import jax
import jax.numpy as jnp
from jax import lax
from jax.sharding import PartitionSpec as P

HEAD_SIZE = 128
MP = 64
MN = 128
KC = 4


NEG_LARGE = -1e30
EPS_NORM = 1e-05


def shifted(block, axis, distance):
    devices = range(lax.axis_size(axis))
    route = [(i - distance, i) for i in devices if i - distance in devices]
    return lax.ppermute(block, axis, route)


def prefix(x, axis, combine, identity):
    length, here = (lax.axis_size(axis), lax.axis_index(axis))
    everything = jax.tree.map(
        lambda part, kind: lax.all_gather(part.astype(kind), axis), x, (jnp.bfloat16, jnp.bfloat16)
    )
    start = jax.tree.map(
        lambda part, zero: jnp.broadcast_to(jnp.asarray(zero, part.dtype), part.shape), x, identity
    )

    def turn(k, before):
        reached = k < here
        new = combine(
            before, jax.tree.map(lambda part, own: part[k].astype(own.dtype), everything, x)
        )
        return jax.tree.map(lambda a, b: jnp.where(reached, a, b), new, before)

    return lax.fori_loop(0, length, turn, start)


def doc_table(doc_lengths):
    return jnp.cumsum(doc_lengths) - doc_lengths


def doc_index(positions, doc_starts):
    return jnp.sum((positions[:, None] >= doc_starts[None, :]).astype(jnp.int32), axis=1) - 1


def allowed_mask(query_pos, key_pos, doc_starts, window_per_head):
    gap = query_pos[:, None] - key_pos[None, :]
    same_doc = doc_index(query_pos, doc_starts)[:, None] == doc_index(key_pos, doc_starts)[None, :]
    base_ok = (gap >= 0) & (key_pos[None, :] >= 0) & same_doc
    return base_ok[None, None] & (gap[None, None] < window_per_head[:, :, None, None])


def attend_piece(
    carry, piece, key_start, grouped_heads, query_pos, doc_starts, window_per_head, reach
):
    key_rows, value_rows = piece
    key_count = key_rows.shape[0]
    shared_heads = grouped_heads.shape[1]
    key_pos = jnp.arange(key_count, dtype=jnp.int32)

    def compute(state):
        old_max, old_total, old_accum = state
        keys_rank3 = key_rows.reshape(key_count, shared_heads, HEAD_SIZE)
        values_rank3 = value_rows.reshape(key_count, shared_heads, HEAD_SIZE)
        scores = jnp.einsum(
            "tgqd,sgd->gqts", grouped_heads, keys_rank3, preferred_element_type=jnp.float32
        ) * (1.0 / math.sqrt(HEAD_SIZE))
        allowed = allowed_mask(query_pos, key_pos, doc_starts, window_per_head)
        scores = jnp.where(allowed, scores, NEG_LARGE)
        new_max = jnp.maximum(old_max, jnp.max(scores, axis=-1))
        weights = jnp.where(allowed, jnp.exp(scores - new_max[..., None]), 0.0)
        new_total = jnp.sum(weights, axis=-1)
        product = jnp.einsum(
            "gqts,sgd->gqtd",
            weights.astype(jnp.bfloat16),
            values_rank3,
            preferred_element_type=jnp.float32,
        )
        return (new_max, new_total, product)

    touches = (key_start + key_count - 1 >= query_pos[0] - reach) & (key_start <= query_pos[-1])
    return lax.cond(touches, compute, lambda state: state, carry)


def causal_conv(extended, taps, positions, doc_starts):
    count = positions.shape[0]
    docs_out = doc_index(positions, doc_starts)
    ext_pos = positions[0] - (KC - 1) + jnp.arange(count + KC - 1, dtype=jnp.int32)
    docs_ext = doc_index(ext_pos, doc_starts)
    running = jnp.zeros((count, extended.shape[1]), jnp.float32)
    for tap_index in range(KC):
        offset = KC - 1 - tap_index
        valid = (docs_ext[offset : offset + count] == docs_out) & (
            ext_pos[offset : offset + count] >= 0
        )
        term = taps[tap_index].astype(jnp.float32)[None, :] * extended[
            offset : offset + count
        ].astype(jnp.float32)
        running = running + jnp.where(valid[:, None], term, 0.0)
    return jax.nn.silu(running).astype(jnp.bfloat16)


def stretch_terms(x_rows, b_rows, c_rows, dt_rows, positions, doc_starts, dt_bias, decay_rate):
    count = positions.shape[0]
    heads = x_rows.shape[1] // MP
    groups = b_rows.shape[1] // MN
    per_group = heads // groups
    docs = doc_index(positions, doc_starts)
    prior_doc = doc_index(positions[:1] - 1, doc_starts)[0]
    delta = jax.nn.softplus(dt_rows.astype(jnp.float32) + dt_bias[None, :])
    log_decay = -delta * decay_rate[None, :]
    running = jnp.cumsum(log_decay, axis=0)
    running_heads = running.T
    order = jnp.arange(count, dtype=jnp.int32)
    causal = order[:, None] >= order[None, :]
    same_doc = docs[:, None] == docs[None, :]
    gaps = running_heads[:, :, None] - running_heads[:, None, :]
    segment = jnp.where((causal & same_doc)[None], jnp.exp(jnp.minimum(gaps, 0.0)), 0.0)
    inputs3 = x_rows.reshape(count, heads, MP)
    b_groups = b_rows.reshape(count, groups, MN)
    c_groups = c_rows.reshape(count, groups, MN)
    cross = jnp.einsum("tgn,sgn->gts", c_groups, b_groups, preferred_element_type=jnp.float32)
    cross_heads = jnp.repeat(cross, per_group, axis=0)
    mixing = (segment * cross_heads * delta.T[:, None, :]).astype(jnp.bfloat16)
    intra = jnp.einsum("hts,shp->thp", mixing, inputs3, preferred_element_type=jnp.float32)
    last_doc = docs[count - 1]
    to_end = (
        jnp.where((docs == last_doc)[:, None], jnp.exp(running[count - 1][None, :] - running), 0.0)
        * delta
    )
    weighted = (inputs3.astype(jnp.float32) * to_end[:, :, None]).astype(jnp.bfloat16)
    b_heads = jnp.repeat(b_groups, per_group, axis=1)
    local_state = jnp.einsum("shp,shn->hpn", weighted, b_heads, preferred_element_type=jnp.float32)
    carry_factor = jnp.where(prior_doc == last_doc, jnp.exp(running[count - 1]), 0.0)
    inflow = jnp.where((docs == prior_doc)[:, None], jnp.exp(running), 0.0)
    c_heads = jnp.repeat(c_groups, per_group, axis=1)
    return (intra, local_state, carry_factor, inflow, c_heads)


def stretch_finish(intra, incoming, inflow, c_heads, x_rows, skip_gain, norm_gain):
    count = x_rows.shape[0]
    heads = x_rows.shape[1] // MP
    incoming_bf = incoming.astype(jnp.bfloat16)
    entering = (
        jnp.einsum("thn,hpn->thp", c_heads, incoming_bf, preferred_element_type=jnp.float32)
        * inflow[:, :, None]
    )
    inputs3 = x_rows.reshape(count, heads, MP).astype(jnp.float32)
    mixed = intra + entering + skip_gain[None, :, None] * inputs3
    mean_square = jnp.mean(mixed * mixed, axis=-1, keepdims=True)
    normed = mixed * lax.rsqrt(mean_square + EPS_NORM) * norm_gain.reshape(heads, MP)[None]
    return normed.reshape(count, heads * MP).astype(jnp.bfloat16)


def combine_states(earlier, later):
    return (earlier[0] * later[0], later[0][:, None, None] * earlier[1] + later[1])


def local(
    queries,
    keys,
    values,
    mamba_x,
    mamba_b,
    mamba_c,
    mamba_dt,
    conv_x,
    conv_b,
    conv_c,
    dt_bias,
    decay_rate,
    skip_gain,
    norm_gain,
    windows,
    doc_lengths,
):
    served = (
        lax.all_to_all(queries, "tensor", split_axis=1, concat_axis=0, tiled=True),
        lax.all_to_all(keys, "tensor", split_axis=1, concat_axis=0, tiled=True),
        lax.all_to_all(values, "tensor", split_axis=1, concat_axis=0, tiled=True),
        lax.all_to_all(mamba_x, "tensor", split_axis=1, concat_axis=0, tiled=True),
        lax.all_to_all(mamba_b, "tensor", split_axis=1, concat_axis=0, tiled=True),
        lax.all_to_all(mamba_c, "tensor", split_axis=1, concat_axis=0, tiled=True),
        lax.all_to_all(mamba_dt, "tensor", split_axis=1, concat_axis=0, tiled=True),
    )
    query_rows, key_rows, value_rows, x_rows, b_rows, c_rows, dt_rows = served
    row_count = query_rows.shape[0]
    shard_start = lax.axis_index("seq") * row_count
    positions = shard_start + jnp.arange(row_count, dtype=jnp.int32)
    doc_starts = doc_table(doc_lengths)
    query_heads = query_rows.shape[1] // HEAD_SIZE
    shared_heads = key_rows.shape[1] // HEAD_SIZE
    group_width = query_heads // shared_heads
    window_per_head = lax.dynamic_slice_in_dim(
        windows, lax.axis_index("tensor") * query_heads, query_heads
    ).reshape(shared_heads, group_width)
    reach = jnp.max(window_per_head)
    grouped_heads = query_rows.reshape(row_count, shared_heads, group_width, HEAD_SIZE)
    initial = (
        jnp.full((shared_heads, group_width, row_count), NEG_LARGE, jnp.float32),
        jnp.zeros((shared_heads, group_width, row_count), jnp.float32),
        jnp.zeros((shared_heads, group_width, row_count, HEAD_SIZE), jnp.float32),
    )
    final = attend_piece(
        initial,
        (
            lax.all_gather(key_rows, "seq", axis=0, tiled=True),
            lax.all_gather(value_rows, "seq", axis=0, tiled=True),
        ),
        jnp.int32(0),
        grouped_heads,
        positions,
        doc_starts,
        window_per_head,
        reach,
    )
    final_max, totals, accum = final
    attention = (
        (accum / totals[..., None])
        .transpose(2, 0, 1, 3)
        .reshape(row_count, query_heads * HEAD_SIZE)
        .astype(jnp.bfloat16)
    )
    edge = row_count - (KC - 1)
    tails = shifted((x_rows[edge:], b_rows[edge:], c_rows[edge:]), "seq", 1)
    conv_x_out = causal_conv(
        jnp.concatenate([tails[0], x_rows], axis=0), conv_x, positions, doc_starts
    )
    conv_b_out = causal_conv(
        jnp.concatenate([tails[1], b_rows], axis=0), conv_b, positions, doc_starts
    )
    conv_c_out = causal_conv(
        jnp.concatenate([tails[2], c_rows], axis=0), conv_c, positions, doc_starts
    )
    intra, local_state, carry_factor, inflow, c_heads = stretch_terms(
        conv_x_out, conv_b_out, conv_c_out, dt_rows, positions, doc_starts, dt_bias, decay_rate
    )
    incoming = prefix(
        (carry_factor, local_state),
        "seq",
        combine_states,
        (jnp.ones_like(carry_factor), jnp.zeros_like(local_state)),
    )
    mamba_out = stretch_finish(
        intra, incoming[1], inflow, c_heads, conv_x_out, skip_gain, norm_gain
    )
    sums = lax.psum(
        (
            jnp.sum(attention.astype(jnp.float32), axis=0),
            jnp.sum(mamba_out.astype(jnp.float32), axis=0),
        ),
        "seq",
    )
    return (attention, mamba_out, sums[0], sums[1])


def solution(mesh):
    placed = (
        P(("seq", "tensor"), None),
        P(("seq", "tensor"), None),
        P(("seq", "tensor"), None),
        P(("seq", "tensor"), None),
        P(("seq", "tensor"), None),
        P(("seq", "tensor"), None),
        P(("seq", "tensor"), None),
        P(None, "tensor"),
        P(None, "tensor"),
        P(None, "tensor"),
        P("tensor"),
        P("tensor"),
        P("tensor"),
        P("tensor"),
        P(),
        P(),
    )
    return jax.shard_map(
        local,
        mesh=mesh,
        in_specs=placed,
        out_specs=(P("seq", "tensor"), P("seq", "tensor"), P("tensor"), P("tensor")),
        check_vma=False,
    )
```

profile of v0, /device:TPU:0, one launch (start us, length us, event | category | flops | bytes accessed | tf_op | source)
XLA Modules:
  0.0 185.0 jit_solution(2254786012537562026)
XLA Ops:
  8.7 6.3 %all-to-all-start.4 = ((bf16[4,2,512]{2,1,0:T(2,128)(2,1)}), bf16[4,2,512]{2,1,0:T(2,128)(2,1)S(1)}, u32[]{:S(2)}, u32[]{:S(2)}) async-start(bf16[4,2,512]{2,1,0:T(2,128)(2,1)} %reshape.408), calls=%async_computation.4 | async-start | bytes 16384 | tf_op jit(solution)/shard_map/all_to_all | solution.py:189
  21.0 1.5 copy.168
  22.5 5.1 %all-to-all-start.6 = ((bf16[32,4,256]{2,0,1:T(8,128)(2,1)}), bf16[32,4,256]{2,0,1:T(8,128)(2,1)S(1)}, u32[]{:S(2)}, u32[]{:S(2)}) async-start(bf16[32,4,256]{2,0,1:T(8,128)(2,1)} %bitcast.129), calls=%async_computation.6 | async-start | bytes 131072 | tf_op jit(solution)/shard_map/all_to_all | solution.py:187
  28.1 1.9 %copy.166 = bf16[4,4,8,2048]{3,2,0,1:T(8,128)(2,1)} copy(bf16[4,4,8,2048]{3,2,1,0:T(8,128)(2,1)} %bitcast.155) | data formatting | bytes 1048576 | tf_op jit(solution)/shard_map/all_to_all | solution.py:186
  30.6 2.7 %all-to-all-done.6 = bf16[32,4,256]{2,0,1:T(8,128)(2,1)S(1)} async-done(((bf16[32,4,256]{2,0,1:T(8,128)(2,1)}), bf16[32,4,256]{2,0,1:T(8,128)(2,1)S(1)}, u32[]{:S(2)}, u32[]{:S(2)}) %all-to-all-start.6) | async-done | bytes 65568 | tf_op jit(solution)/shard_map/all_to_all | solution.py:187
  33.3 3.6 %all-to-all-start.3 = ((bf16[32,4,2048]{2,0,1:T(8,128)(2,1)}), bf16[32,4,2048]{2,0,1:T(8,128)(2,1)S(1)}, u32[]{:S(2)}, u32[]{:S(2)}) async-start(bf16[32,4,2048]{2,0,1:T(8,128)(2,1)} %bitcast.127), calls=%async_computation.3 | async-start | bytes 1048576 | tf_op jit(solution)/shard_map/all_to_all | solution.py:186
  41.5 8.2 %all-to-all-done.3 = bf16[32,4,2048]{2,0,1:T(8,128)(2,1)S(1)} async-done(((bf16[32,4,2048]{2,0,1:T(8,128)(2,1)}), bf16[32,4,2048]{2,0,1:T(8,128)(2,1)S(1)}, u32[]{:S(2)}, u32[]{:S(2)}) %all-to-all-start.3) | async-done | bytes 524320 | tf_op jit(solution)/shard_map/all_to_all | solution.py:186
  55.2 3.3 %all-to-all-start.5 = ((bf16[32,4,256]{2,0,1:T(8,128)(2,1)}), bf16[32,4,256]{2,0,1:T(8,128)(2,1)S(1)}, u32[]{:S(2)}, u32[]{:S(2)}) async-start(bf16[32,4,256]{2,0,1:T(8,128)(2,1)} %bitcast.130), calls=%async_computation.5 | async-start | bytes 131072 | tf_op jit(solution)/shard_map/all_to_all | solution.py:188
  61.3 2.9 %all-to-all-done.5 = bf16[32,4,256]{2,0,1:T(8,128)(2,1)S(1)} async-done(((bf16[32,4,256]{2,0,1:T(8,128)(2,1)}), bf16[32,4,256]{2,0,1:T(8,128)(2,1)S(1)}, u32[]{:S(2)}, u32[]{:S(2)}) %all-to-all-start.5) | async-done | bytes 65568 | tf_op jit(solution)/shard_map/all_to_all | solution.py:188
  64.2 3.3 %all-to-all-start = ((bf16[32,4,256]{2,0,1:T(8,128)(2,1)}), bf16[32,4,256]{2,0,1:T(8,128)(2,1)S(1)}, u32[]{:S(2)}, u32[]{:S(2)}) async-start(bf16[32,4,256]{2,0,1:T(8,128)(2,1)} %bitcast.132), calls=%async_computation | async-start | bytes 131072 | tf_op jit(solution)/shard_map/all_to_all | solution.py:184
  70.8 12.8 %all-gather.1 = bf16[8,1,32]{2,1,0:T(2,128)(2,1)S(1)} all-gather(bf16[1,1,32]{2,1,0:T(2,128)(2,1)S(1)} %get-tuple-element.210), channel_id=1, replica_groups=mesh['seq'=8,'tensor'=4] {'seq'}, dimensions={0}, use_global_device_ids=true | all-gather | bytes 576 | tf_op jit(solution)/shard_map/all_gather | solution.py:27
  85.0 2.2 %collective-permute-start.1 = (bf16[3,256]{1,0:T(4,128)(2,1)S(1)}, bf16[3,256]{1,0:T(4,128)(2,1)S(1)}, u32[]{:S(2)}, u32[]{:S(2)}) collective-permute-start(bf16[3,256]{1,0:T(4,128)(2,1)S(1)} %slice.170), channel_id=1, source_target_pairs={{0,4},{4,8},{8,12},{12,16},{16,20},{20,24},{24,28},{1,5},{5,9},{9,... | collective-permute-start | bytes 4616 | tf_op jit(solution)/shard_map/ppermute | solution.py:21
  87.2 5.1 %all-to-all-start.2 = ((bf16[32,4,256]{2,0,1:T(8,128)(2,1)}), bf16[32,4,256]{2,0,1:T(8,128)(2,1)S(1)}, u32[]{:S(2)}, u32[]{:S(2)}) async-start(bf16[32,4,256]{2,0,1:T(8,128)(2,1)} %bitcast.131), calls=%async_computation.2 | async-start | bytes 131072 | tf_op jit(solution)/shard_map/all_to_all | solution.py:185
  92.3 9.3 %all_gather.16 = bf16[1024,256]{1,0:T(8,128)(2,1)S(1)} all-gather(bf16[128,256]{1,0:T(8,128)(2,1)S(1)} %bitcast.162), channel_id=1, replica_groups=mesh['seq'=8,'tensor'=4] {'seq'}, dimensions={0}, use_global_device_ids=true | all-gather | bytes 589824 | tf_op jit(solution)/shard_map/all_gather | solution.py:212
  101.6 4.7 %all-to-all-start.1 = ((bf16[32,4,1024]{2,0,1:T(8,128)(2,1)}), bf16[32,4,1024]{2,0,1:T(8,128)(2,1)S(1)}, u32[]{:S(2)}, u32[]{:S(2)}) async-start(bf16[32,4,1024]{2,0,1:T(8,128)(2,1)} %bitcast.128), calls=%async_computation.1 | async-start | bytes 524288 | tf_op jit(solution)/shard_map/all_to_all | solution.py:183
  106.3 9.7 %all_gather.17 = bf16[1024,256]{1,0:T(8,128)(2,1)S(1)} all-gather(bf16[128,256]{1,0:T(8,128)(2,1)S(1)} %bitcast.163), channel_id=1, replica_groups=mesh['seq'=8,'tensor'=4] {'seq'}, dimensions={0}, use_global_device_ids=true | all-gather | bytes 589824 | tf_op jit(solution)/shard_map/all_gather | solution.py:213
  117.3 1.6 fusion.13
  118.9 13.4 %conditional.1 = (f32[2,4,128]{2,1,0:T(4,128)S(1)}, f32[2,4,128,128]{3,2,1,0:T(8,128)S(1)}) conditional(s32[]{:T(128)} %convert_element_type.180, () %tuple.30, (s32[128]{0:T(128)S(1)}, s32[1024]{0:T(1024)S(1)}, s32[1024]{0:T(1024)S(1)}, s32[3]{0:T(128)S(1)}, s32[1024]{0:T(1024)S(1)}, /*index=5*/s32[8]{0:T(128)}, bf16[1024,256]{1,0:T(8,128)(2,1)S(1)}, ...), branch_computations={%region_2.3_spmd, %region_3.8_spmd} | conditional | flops 557590656 | bytes 36501220 | solution.py:87
  122.0 4.1 %fusion = (f32[2,4,128]{2,1,0:T(4,128)S(1)}, f32[2,1024,128,4]{2,1,3,0:T(8,128)}) fusion(s32[2,4]{1,0:T(2,128)S(1)} %lt.30, s32[128,1024]{0,1:T(8,128)S(1)} %broadcast_subtract_fusion, pred[128,1024]{0,1:T(8,128)(4,1)S(1)} %compare_and_fusion.1, bf16[128,2,4,128]{3,2,1,0:T(4,128)(2,1)S(1)} %reshape.368, bf16[1024,2,128,1]{2,1,0,3:T(2,128)(2,1)} %bitcast.156), kind=kOutput, calls=%fused_computation.3 | convolution fusion | flops 273677312 | bytes 5640224 | tf_op jit(solution)/shard_map/cond/branch_1_fun/tgqd,sgd->gqts/dot_general | solution.py:70
  126.3 4.3 %fusion.1 = f32[2,4,128,128]{3,2,1,0:T(8,128)S(1)} fusion(f32[2,1024,128,4]{2,1,3,0:T(8,128)} %get-tuple-element.206, f32[2,4,128]{2,1,0:T(4,128)S(1)} %broadcast_maximum_fusion, s32[2,4]{1,0:T(2,128)S(1)} %lt.30, s32[128,1024]{0,1:T(8,128)S(1)} %broadcast_subtract_fusion, pred[128,1024]{0,1:T(8,128)(4,1)S(1)} %compare_and_fusion.1, ...), kind=kOutput, calls=%fused_computation.4 | convolution fusion | flops 275775488 | bytes 5902368 | tf_op jit(solution)/shard_map/cond/branch_1_fun/gqts,sgd->gqtd/dot_general | solution.py:78
  130.6 1.6 fusion.3
  133.5 2.0 %convolution_bitcast_fusion.1 = f32[128,32,64]{0,2,1:T(8,128)S(1)} fusion(bf16[128,32,64]{0,2,1:T(8,128)(2,1)S(1)} %bitcast.140, bf16[32,128,128]{2,1,0:T(8,128)(2,1)} %fusion.13), kind=kOutput, calls=%fused_computation.32 | convolution fusion | flops 67108864 | bytes 2621440 | tf_op jit(solution)/shard_map/hts,shp->thp/dot_general | solution.py:130
  135.6 16.0 %while.14 = (s32[]{:T(128)}, f32[32,64,128]{2,1,0:T(8,128)S(1)}, s32[]{:T(128)}, bf16[8,32]{1,0:T(8,128)(2,1)}, bf16[8,32,64,128]{3,2,1,0:T(8,128)(2,1)}, /*index=5*/s32[]{:T(128)}, s32[]{:T(128)}) while((s32[]{:T(128)}, f32[32,64,128]{2,1,0:T(8,128)S(1)}, s32[]{:T(128)}, bf16[8,32]{1,0:T(8,128)(2,1)}, ...), condition=%wide.region_13.14_spmd.clone, body=%wide.region_12.13_spmd.clone.sunk | while | flops 1310756 | bytes 2621865 | solution.py:40
  154.6 23.6 %all-reduce = (f32[1024]{0:T(1024)}, f32[2048]{0:T(1024)}) all-reduce(f32[1024]{0:T(1024)S(1)} %bitcast.175, f32[2048]{0:T(1024)S(1)} %reduce_sum.112), channel_id=1, replica_groups=mesh['seq'=8,'tensor'=4] {'seq'}, use_global_device_ids=true, to_apply=%region_16.17 | all-reduce | flops 3072 | bytes 24576 | tf_op jit(solution)/shard_map/psum | solution.py:252
  (123 shorter events, 46.0 us)
Async XLA Ops:
  8.7 13.8 %all-to-all-start.4 = ((bf16[4,2,512]{2,1,0:T(2,128)(2,1)}), bf16[4,2,512]{2,1,0:T(2,128)(2,1)S(1)}, u32[]{:S(2)}, u32[]{:S(2)}) async-start(bf16[4,2,512]{2,1,0:T(2,128)(2,1)} %reshape.408), calls=%async_computation.4 | async-start | bytes 16384 | tf_op jit(solution)/shard_map/all_to_all | solution.py:189
  22.5 10.8 %all-to-all-start.6 = ((bf16[32,4,256]{2,0,1:T(8,128)(2,1)}), bf16[32,4,256]{2,0,1:T(8,128)(2,1)S(1)}, u32[]{:S(2)}, u32[]{:S(2)}) async-start(bf16[32,4,256]{2,0,1:T(8,128)(2,1)} %bitcast.129), calls=%async_computation.6 | async-start | bytes 131072 | tf_op jit(solution)/shard_map/all_to_all | solution.py:187
  30.0 24.6 %copy-start.5 = (bf16[32,1024]{1,0:T(8,128)(2,1)S(1)}, bf16[32,1024]{1,0:T(8,128)(2,1)}, u32[]{:S(2)}) copy-start(bf16[32,1024]{1,0:T(8,128)(2,1)} %param.25) | copy-start | bytes 196612
  33.3 25.3 %copy-start.9 = (bf16[4,256]{1,0:T(4,128)(2,1)S(1)}, bf16[4,256]{1,0:T(4,128)(2,1)}, u32[]{:S(2)}) copy-start(bf16[4,256]{1,0:T(4,128)(2,1)} %param.29) | copy-start | bytes 6148
  33.3 25.3 %copy-start.8 = (f32[2048]{0:T(1024)S(1)}, f32[2048]{0:T(1024)}, u32[]{:S(2)}) copy-start(f32[2048]{0:T(1024)} %param.33) | copy-start | bytes 24580
  33.3 26.0 %copy-start.6 = (bf16[32,1024]{1,0:T(8,128)(2,1)S(1)}, bf16[32,1024]{1,0:T(8,128)(2,1)}, u32[]{:S(2)}) copy-start(bf16[32,1024]{1,0:T(8,128)(2,1)} %param.21) | copy-start | bytes 196612
  33.3 26.6 %copy-start.7 = (bf16[32,1024]{1,0:T(8,128)(2,1)S(1)}, bf16[32,1024]{1,0:T(8,128)(2,1)}, u32[]{:S(2)}) copy-start(bf16[32,1024]{1,0:T(8,128)(2,1)} %param.22) | copy-start | bytes 196612
  33.3 27.2 %copy-start.2 = (bf16[32,4096]{1,0:T(8,128)(2,1)S(1)}, bf16[32,4096]{1,0:T(8,128)(2,1)}, u32[]{:S(2)}) copy-start(bf16[32,4096]{1,0:T(8,128)(2,1)} %param.20) | copy-start | bytes 786436
  33.3 16.4 %all-to-all-start.3 = ((bf16[32,4,2048]{2,0,1:T(8,128)(2,1)}), bf16[32,4,2048]{2,0,1:T(8,128)(2,1)S(1)}, u32[]{:S(2)}, u32[]{:S(2)}) async-start(bf16[32,4,2048]{2,0,1:T(8,128)(2,1)} %bitcast.127), calls=%async_computation.3 | async-start | bytes 1048576 | tf_op jit(solution)/shard_map/all_to_all | solution.py:186
  36.9 30.6 %copy-start.11 = (s32[32]{0:T(128)S(1)}, s32[32]{0:T(128)}, u32[]{:S(2)}) copy-start(s32[32]{0:T(128)} %param.34) | copy-start | bytes 388
  37.0 98.6 %all-gather.4.cloned.1.call-start = ((), (), s32[]{:S(2)}) async-start(), calls=%async_computation.7 | async-start | bytes 4718592 | tf_op jit(solution)/shard_map/all_gather | solution.py:27
  39.4 11.6 %collective-permute-start.2 = (bf16[3,256]{1,0:T(4,128)(2,1)S(1)}, bf16[3,256]{1,0:T(4,128)(2,1)S(1)}, u32[]{:S(2)}, u32[]{:S(2)}) collective-permute-start(bf16[3,256]{1,0:T(4,128)(2,1)S(1)} %slice.175), channel_id=1, source_target_pairs={{0,4},{4,8},{8,12},{12,16},{16,20},{20,24},{24,28},{1,5},{5,9},{9,... | collective-permute-start | bytes 4616 | tf_op jit(solution)/shard_map/ppermute | solution.py:21
  49.7 2.1 %collective-permute-start = (bf16[3,2048]{1,0:T(4,128)(2,1)S(1)}, bf16[3,2048]{1,0:T(4,128)(2,1)S(1)}, u32[]{:S(2)}, u32[]{:S(2)}) collective-permute-start(bf16[3,2048]{1,0:T(4,128)(2,1)S(1)} %slice.165), channel_id=1, source_target_pairs={{0,4},{4,8},{8,12},{12,16},{16,20},{20,24},{24,28},{1,5},{5,9},{9,... | collective-permute-start | bytes 36872 | tf_op jit(solution)/shard_map/ppermute | solution.py:21
  55.2 9.0 %all-to-all-start.5 = ((bf16[32,4,256]{2,0,1:T(8,128)(2,1)}), bf16[32,4,256]{2,0,1:T(8,128)(2,1)S(1)}, u32[]{:S(2)}, u32[]{:S(2)}) async-start(bf16[32,4,256]{2,0,1:T(8,128)(2,1)} %bitcast.130), calls=%async_computation.5 | async-start | bytes 131072 | tf_op jit(solution)/shard_map/all_to_all | solution.py:188
  64.2 23.0 %all-to-all-start = ((bf16[32,4,256]{2,0,1:T(8,128)(2,1)}), bf16[32,4,256]{2,0,1:T(8,128)(2,1)S(1)}, u32[]{:S(2)}, u32[]{:S(2)}) async-start(bf16[32,4,256]{2,0,1:T(8,128)(2,1)} %bitcast.132), calls=%async_computation | async-start | bytes 131072 | tf_op jit(solution)/shard_map/all_to_all | solution.py:184
  85.0 31.1 %collective-permute-start.1 = (bf16[3,256]{1,0:T(4,128)(2,1)S(1)}, bf16[3,256]{1,0:T(4,128)(2,1)S(1)}, u32[]{:S(2)}, u32[]{:S(2)}) collective-permute-start(bf16[3,256]{1,0:T(4,128)(2,1)S(1)} %slice.170), channel_id=1, source_target_pairs={{0,4},{4,8},{8,12},{12,16},{16,20},{20,24},{24,28},{1,5},{5,9},{9,... | collective-permute-start | bytes 4616 | tf_op jit(solution)/shard_map/ppermute | solution.py:21
  87.2 14.4 %all-to-all-start.2 = ((bf16[32,4,256]{2,0,1:T(8,128)(2,1)}), bf16[32,4,256]{2,0,1:T(8,128)(2,1)S(1)}, u32[]{:S(2)}, u32[]{:S(2)}) async-start(bf16[32,4,256]{2,0,1:T(8,128)(2,1)} %bitcast.131), calls=%async_computation.2 | async-start | bytes 131072 | tf_op jit(solution)/shard_map/all_to_all | solution.py:185
  101.6 17.3 %all-to-all-start.1 = ((bf16[32,4,1024]{2,0,1:T(8,128)(2,1)}), bf16[32,4,1024]{2,0,1:T(8,128)(2,1)S(1)}, u32[]{:S(2)}, u32[]{:S(2)}) async-start(bf16[32,4,1024]{2,0,1:T(8,128)(2,1)} %bitcast.128), calls=%async_computation.1 | async-start | bytes 524288 | tf_op jit(solution)/shard_map/all_to_all | solution.py:183
  126.3 4.4 %copy-start = (f32[2,1024,128,4]{2,1,3,0:T(8,128)S(1)}, f32[2,1024,128,4]{2,1,3,0:T(8,128)}, u32[]{:S(2)}) copy-start(f32[2,1024,128,4]{2,1,3,0:T(8,128)} %get-tuple-element.206) | copy-start | bytes 12582916 | tf_op jit(solution)/shard_map/cond
  135.6 16.1 %copy-start.1 = (bf16[128,2,128]{2,0,1:T(8,128)(2,1)S(1)}, bf16[128,2,128]{2,0,1:T(8,128)(2,1)}, u32[]{:S(2)}) copy-start(bf16[128,2,128]{2,0,1:T(8,128)(2,1)} %copy.129) | copy-start | bytes 196612
  135.6 16.3 %copy-start.3 = (f32[128,32]{0,1:T(8,128)S(1)}, f32[128,32]{0,1:T(8,128)}, u32[]{:S(2)}) copy-start(f32[128,32]{0,1:T(8,128)} %copy.130) | copy-start | bytes 49156
  135.6 16.3 %copy-start.10 = (f32[32]{0:T(128)S(1)}, f32[32]{0:T(128)}, u32[]{:S(2)}) copy-start(f32[32]{0:T(128)} %param.32) | copy-start | bytes 388
  151.7 1.2 copy-start.4
Sparse Core Ops, SparseCore 0:
  54.7 38.6 all-gather.3
where the time goes:
time: 187 us; the launch traced here: 185 us
  blocking collectives  55.4 us (30%)
  starting transfers between devices  36.3 us (19%)
  other arithmetic  30.3 us (16%)
  between operations  19 us (10%)
  local copies, waits for them, and re-layouts  16.8 us (9%)
  waiting for transfers between devices  14.2 us (8%)
  matrix products  12.8 us (7%)
    psum x1, blocking collectives, local(): lax.psum((jnp.sum(attention.astype(jnp.float32), axis=0), jnp.sum(mamba_o...  23.6 us
    all_gather x1, blocking collectives, prefix(): lax.all_gather(part.astype(kind), axis)  12.8 us
    select_n x8, other arithmetic, turn(): return jax.tree.map(lambda a, b: jnp.where(reached, a, b), new, before)  10.4 us
    all_gather x1, blocking collectives, local(): lax.all_gather(value_rows, 'seq', axis=0, tiled=True)  9.74 us
    all_gather x1, blocking collectives, local(): lax.all_gather(key_rows, 'seq', axis=0, tiled=True)  9.29 us
    all_to_all x1, waiting for transfers between devices, local(): lax.all_to_all(mamba_x, 'tensor', split_axis=1, concat_axis=0, tiled=True)  8.17 us
    all_to_all x1, starting transfers between devices, local(): lax.all_to_all(mamba_dt, 'tensor', split_axis=1, concat_axis=0, tiled=True)  6.35 us
    convert_element_type x8, other arithmetic, turn(): part[k].astype(own.dtype)  5.54 us
  transfers between devices with their start and end apart: 11, of which 4 were waited for; matrix products, arithmetic and copies ran while one was open for 20% of the time, Pallas kernels for 0%

commit v1 on v0

v1 whole, which is shorter than its diff:
```python
import functools
import math

import jax
import jax.numpy as jnp
from jax import lax
from jax.experimental import pallas as pl
from jax.experimental.pallas import tpu as pltpu
from jax.sharding import Mesh, PartitionSpec as P

HEAD_SIZE = 128
MP = 64
MN = 128
KC = 4
HALO = 8
NEG_LARGE = -1e30
EPS_NORM = 1e-05
PAIR = 2

F32 = jnp.float32
BF16 = jnp.bfloat16


def doc_count(pos, lengths_ref):
    start = jnp.int32(0)
    count = jnp.zeros(pos.shape, jnp.int32) if not isinstance(pos, int) else jnp.int32(0)
    for k in range(lengths_ref.shape[0]):
        count = count + jnp.where(pos >= start, 1, 0)
        start = start + lengths_ref[k]
    return count


def doc_scalar(pos, lengths_ref):
    start = jnp.int32(0)
    count = jnp.int32(0)
    for k in range(lengths_ref.shape[0]):
        count = count + (pos >= start).astype(jnp.int32)
        start = start + lengths_ref[k]
    return count


def softplus(x):
    return jnp.maximum(x, 0.0) + jnp.log1p(jnp.exp(-jnp.abs(x)))


def pair_lanes(first, second, rows):
    lane = lax.broadcasted_iota(jnp.int32, (rows, 2 * MP), 1)
    return jnp.where(lane < MP, first, second)


def pre_kernel(ids, lengths, rows_ref, halo_ref, taps_ref, prow_ref, conv_ref, pay_ref, cum_ref, ext):
    tokens = rows_ref.shape[0]
    width = taps_ref.shape[1]
    heads = prow_ref.shape[1]
    xw = width - 2 * MN
    first = ids[0] * tokens
    pos = first + lax.broadcasted_iota(jnp.int32, (tokens, 1), 0)
    here = doc_count(pos, lengths)
    same = [(doc_count(pos - j, lengths) == here).astype(F32) for j in range(1, KC)]
    step = 2 * MP
    for c in range(0, width, step):
        ext[0:HALO, :] = halo_ref[:, c : c + step].astype(F32)
        ext[HALO : HALO + tokens, :] = rows_ref[:, c : c + step].astype(F32)
        taps = taps_ref[:, c : c + step].astype(F32)
        u = taps[0:1, :] * ext[HALO : HALO + tokens, :]
        for j in range(1, KC):
            u = u + (taps[j : j + 1, :] * ext[HALO - j : HALO - j + tokens, :]) * same[j - 1]
        conv_ref[:, c : c + step] = (u / (1.0 + jnp.exp(-u))).astype(BF16)
    delta = softplus(rows_ref[:, width : width + heads].astype(F32) + prow_ref[0:1, :])
    logd = -delta * prow_ref[1:2, :]
    r = lax.broadcasted_iota(jnp.int32, (tokens, tokens), 0)
    s = lax.broadcasted_iota(jnp.int32, (tokens, tokens), 1)
    cum = jnp.dot(
        (r >= s).astype(F32), logd, precision=lax.Precision.HIGHEST, preferred_element_type=F32
    )
    cum_ref[...] = cum
    last_doc = doc_scalar(first + tokens - 1, lengths)
    to_end = jnp.where(here == last_doc, jnp.exp(cum[tokens - 1 : tokens, :] - cum), 0.0) * delta
    bc = conv_ref[:, xw : xw + MN]
    for k in range(heads // 2):
        weighted = (
            conv_ref[:, k * step : (k + 1) * step].astype(F32)
            * pair_lanes(to_end[:, 2 * k : 2 * k + 1], to_end[:, 2 * k + 1 : 2 * k + 2], tokens)
        ).astype(BF16)
        state = lax.dot_general(
            weighted, bc, (((0,), (0,)), ((), ())), preferred_element_type=F32
        )
        pay_ref[k * step : (k + 1) * step, :] = state.astype(BF16)
    ones = jnp.ones((tokens, MN), F32)
    total = lax.dot_general(
        logd, ones, (((0,), (0,)), ((), ())), precision=lax.Precision.HIGHEST,
        preferred_element_type=F32,
    )
    high = total.astype(BF16)
    pay_ref[xw : xw + heads, :] = high
    pay_ref[xw + heads : xw + 2 * heads, :] = (total - high.astype(F32)).astype(BF16)


def intra_kernel(ids, lengths, rows_ref, conv_ref, cum_ref, prow_ref, pcol_ref, out_ref):
    tokens = rows_ref.shape[0]
    heads = prow_ref.shape[1]
    xw = heads * MP
    half = tokens // PAIR
    step = 2 * MP
    dt = rows_ref[:, xw + 2 * MN : xw + 2 * MN + heads]
    eye = (
        lax.broadcasted_iota(jnp.int32, (heads, heads), 0)
        == lax.broadcasted_iota(jnp.int32, (heads, heads), 1)
    ).astype(BF16)
    dt_t = lax.dot_general(eye, dt, (((1,), (1,)), ((), ())), preferred_element_type=F32)
    delta_t = softplus(dt_t + pcol_ref[:, 0:1])
    logd_t = -delta_t * pcol_ref[:, 1:2]
    r = lax.broadcasted_iota(jnp.int32, (tokens, tokens), 0)
    s = lax.broadcasted_iota(jnp.int32, (tokens, tokens), 1)
    cum_t = jnp.dot(
        logd_t, (r <= s).astype(F32), precision=lax.Precision.HIGHEST, preferred_element_type=F32
    )
    first = ids[0] * tokens
    for b in range(PAIR):
        top, end = b * half, (b + 1) * half
        rpos = first + top + lax.broadcasted_iota(jnp.int32, (half, 1), 0)
        cpos = first + lax.broadcasted_iota(jnp.int32, (1, end), 1)
        allowed = (rpos >= cpos) & (doc_count(rpos, lengths) == doc_count(cpos, lengths))
        cross = lax.dot_general(
            conv_ref[top:end, xw + MN : xw + 2 * MN],
            conv_ref[0:end, xw : xw + MN],
            (((1,), (1,)), ((), ())),
            preferred_element_type=F32,
        )
        cross = jnp.where(allowed, cross, 0.0)
        lane = lax.broadcasted_iota(jnp.int32, (half, step), 1)
        for k in range(heads // 2):
            inputs = conv_ref[0:end, k * step : (k + 1) * step]
            parts = []
            for h in (2 * k, 2 * k + 1):
                gaps = cum_ref[top:end, h : h + 1] - cum_t[h : h + 1, 0:end]
                mix = cross * jnp.exp(jnp.minimum(gaps, 0.0)) * delta_t[h : h + 1, 0:end]
                parts.append(jnp.dot(mix.astype(BF16), inputs, preferred_element_type=F32))
            skip = jnp.where(
                lane < MP, prow_ref[2:3, 2 * k : 2 * k + 1], prow_ref[2:3, 2 * k + 1 : 2 * k + 2]
            )
            own = conv_ref[top:end, k * step : (k + 1) * step].astype(F32)
            out_ref[top:end, k * step : (k + 1) * step] = (
                jnp.where(lane < MP, parts[0], parts[1]) + skip * own
            )


def finish_kernel(count, ids, lengths, *refs):
    pays = refs[:count]
    intra_ref, conv_ref, cum_ref, gain_ref, own_ref, other_ref, sum_ref, full = refs[count:]
    tokens = intra_ref.shape[0]
    heads = cum_ref.shape[1]
    xw = heads * MP
    step = 2 * MP
    half = tokens // PAIR
    first = ids[0] * tokens
    incoming = jnp.zeros((heads, MP, MN), F32)
    total = jnp.zeros((heads, MN), F32)
    prior_doc = doc_scalar(first - 1, lengths)
    for d in range(1, count + 1):
        pay = pays[d - 1]
        reached = (doc_scalar(first - (d - 1) * tokens - 1, lengths) == prior_doc).astype(F32)
        weight = jnp.exp(total) * reached
        incoming = incoming + pay[0:xw, :].astype(F32).reshape(heads, MP, MN) * weight[:, None, :]
        total = (
            total
            + pay[xw : xw + heads, :].astype(F32)
            + pay[xw + heads : xw + 2 * heads, :].astype(F32)
        )
    state = incoming.reshape(xw, MN).astype(BF16)
    pos = first + lax.broadcasted_iota(jnp.int32, (tokens, 1), 0)
    inflow = jnp.where(doc_count(pos, lengths) == prior_doc, jnp.exp(cum_ref[...]), 0.0)
    cc = conv_ref[:, xw + MN : xw + 2 * MN]
    same_head = (
        lax.broadcasted_iota(jnp.int32, (step, step), 0) // MP
        == lax.broadcasted_iota(jnp.int32, (step, step), 1) // MP
    )
    mean = jnp.where(same_head, 1.0 / MP, 0.0).astype(BF16)
    for k in range(heads // 2):
        cols = slice(k * step, (k + 1) * step)
        entering = lax.dot_general(
            cc, state[cols, :], (((1,), (1,)), ((), ())), preferred_element_type=F32
        )
        mixed = intra_ref[:, cols] + entering * pair_lanes(
            inflow[:, 2 * k : 2 * k + 1], inflow[:, 2 * k + 1 : 2 * k + 2], tokens
        )
        square = mixed * mixed
        high = square.astype(BF16)
        low = (square - high.astype(F32)).astype(BF16)
        mean_square = jnp.dot(high, mean, preferred_element_type=F32) + jnp.dot(
            low, mean, preferred_element_type=F32
        )
        normed = (mixed * lax.rsqrt(mean_square + EPS_NORM) * gain_ref[0:1, cols]).astype(BF16)
        sum_ref[:, cols] = jnp.sum(normed.astype(F32), axis=0, keepdims=True)
        full[:, cols] = normed
    split_tokens(ids, full, own_ref, other_ref, half)


def split_tokens(ids, full, own_ref, other_ref, half):
    @pl.when(ids[1] == 0)
    def _():
        own_ref[...] = full[0:half, :]
        other_ref[...] = full[half:, :]

    @pl.when(ids[1] != 0)
    def _():
        own_ref[...] = full[half:, :]
        other_ref[...] = full[0:half, :]


def attention_kernel(ids, lengths, windows, rows_ref, kv_ref, own_ref, other_ref, sum_ref, full, top, den, acc):
    tokens = rows_ref.shape[0]
    shared = kv_ref.shape[2] // (2 * HEAD_SIZE)
    heads = full.shape[1] // HEAD_SIZE
    per = heads // shared
    half = tokens // PAIR
    qw = heads * HEAD_SIZE
    first = ids[0] * tokens
    base = ids[2]
    widest = windows[base]
    for h in range(1, heads):
        widest = jnp.maximum(widest, windows[base + h])
    qpos = first + lax.broadcasted_iota(jnp.int32, (tokens, 1), 0)
    qdoc = doc_count(qpos, lengths)
    ones = jnp.ones((tokens, HEAD_SIZE), BF16)
    scale = 1.0 / math.sqrt(HEAD_SIZE)

    def piece(d, keys, values, start):
        kpos = (first - d * tokens) + lax.broadcasted_iota(jnp.int32, (1, tokens), 1)
        gap = qpos - kpos
        ok = (gap >= 0) & (kpos >= 0) & (qdoc == doc_count(kpos, lengths))
        for h in range(heads):
            cols = slice(h * HEAD_SIZE, (h + 1) * HEAD_SIZE)
            g = (h // per) * HEAD_SIZE
            scores = lax.dot_general(
                rows_ref[:, cols], keys(g), (((1,), (1,)), ((), ())), preferred_element_type=F32
            ) * scale
            allowed = ok & (gap < windows[base + h])
            scores = jnp.where(allowed, scores, NEG_LARGE)
            now = jnp.max(scores, axis=1, keepdims=True)
            if not start:
                before = top[:, h : h + 1]
                now = jnp.maximum(now, before)
                fade = jnp.exp(before - now)
            weights = jnp.where(allowed, jnp.exp(scores - now), 0.0)
            total = jnp.sum(weights, axis=1, keepdims=True)
            product = jnp.dot(weights.astype(BF16), values(g), preferred_element_type=F32)
            top[:, h : h + 1] = now
            if start:
                den[:, h : h + 1] = total
                acc[:, cols] = product
            else:
                den[:, h : h + 1] = den[:, h : h + 1] * fade + total
                acc[:, cols] = acc[:, cols] * fade + product

    kw = shared * HEAD_SIZE
    piece(
        0,
        lambda g: rows_ref[:, qw + g : qw + g + HEAD_SIZE],
        lambda g: rows_ref[:, qw + kw + g : qw + kw + g + HEAD_SIZE],
        True,
    )
    first_doc = doc_scalar(first, lengths)

    def turn(d, carry):
        end = first - (d - 1) * tokens - 1
        touches = (end >= 0) & (first - end < widest) & (doc_scalar(end, lengths) == first_doc)

        @pl.when(touches)
        def _():
            piece(
                d,
                lambda g: kv_ref[d - 1, :, g : g + HEAD_SIZE],
                lambda g: kv_ref[d - 1, :, kw + g : kw + g + HEAD_SIZE],
                False,
            )

        return carry

    lax.fori_loop(1, kv_ref.shape[0] + 1, turn, 0)
    for h in range(heads):
        cols = slice(h * HEAD_SIZE, (h + 1) * HEAD_SIZE)
        result = (acc[:, cols] / den[:, h : h + 1]).astype(BF16)
        sum_ref[:, cols] = jnp.sum(result.astype(F32), axis=0, keepdims=True)
        full[:, cols] = result
    split_tokens(ids, full, own_ref, other_ref, half)


SMEM = pl.BlockSpec(memory_space=pltpu.SMEM)
VMEM = pl.BlockSpec(memory_space=pltpu.VMEM)


def call(kernel, scalars, arrays, outs, scratch=(), name=None):
    return pl.pallas_call(
        kernel,
        out_shape=[jax.ShapeDtypeStruct(shape, dtype) for shape, dtype in outs],
        in_specs=[SMEM] * len(scalars) + [VMEM] * len(arrays),
        out_specs=[VMEM] * len(outs),
        scratch_shapes=list(scratch),
        name=name,
    )(*scalars, *arrays)


def pack(parts, tensor):
    rows = parts[0].shape[0]
    split = [p.reshape(rows, tensor, PAIR, p.shape[1] // (tensor * PAIR)) for p in parts]
    joined = jnp.concatenate(split, axis=3)
    return joined.transpose(2, 1, 0, 3).reshape(PAIR * tensor, rows, joined.shape[3])


def to_heads(parts, tensor):
    packed = pack(parts, tensor)
    moved = lax.all_to_all(packed, ("core", "tensor"), split_axis=0, concat_axis=0, tiled=True)
    return moved.reshape(moved.shape[0] * moved.shape[1], moved.shape[2])


def earlier(block, chips):
    return [
        lax.ppermute(block, "chip", [(i, i + d) for i in range(chips - d)])
        for d in range(1, chips)
    ]


def half_columns(x, core):
    width = x.shape[-1] // PAIR
    return lax.dynamic_slice_in_dim(x, core * width, width, x.ndim - 1)


def swap(x):
    return lax.ppermute(x, "core", [(0, 1), (1, 0)])


def join(core, own, received):
    return jnp.where(
        core == 0,
        jnp.concatenate([own, received], axis=1),
        jnp.concatenate([received, own], axis=1),
    )


def local(
    queries, keys, values, mamba_x, mamba_b, mamba_c, mamba_dt, conv_x, conv_b, conv_c,
    dt_bias, decay_rate, skip_gain, norm_gain, windows, doc_lengths,
):
    chips = lax.axis_size("chip")
    tensor = lax.axis_size("tensor")
    core = lax.axis_index("core")
    chip = lax.axis_index("chip")
    q_heads = queries.shape[1] // HEAD_SIZE // (tensor * PAIR)
    base = (lax.axis_index("tensor") * PAIR + core) * q_heads
    ids = jnp.stack([chip, core, base]).astype(jnp.int32)

    rows = to_heads((mamba_x, mamba_b, mamba_c, mamba_dt), tensor)
    qkv = to_heads((queries, keys, values), tensor)
    tokens = rows.shape[0]
    half = tokens // PAIR
    taps = jnp.concatenate([half_columns(c, core) for c in (conv_x, conv_b, conv_c)], axis=1)
    width = taps.shape[1]
    halo = lax.ppermute(
        rows[tokens - HALO :, :width], "chip", [(i, i + 1) for i in range(chips - 1)]
    )
    prow = half_columns(jnp.stack([dt_bias, decay_rate, skip_gain]), core)
    pcol = prow.T
    gain = half_columns(norm_gain[None, :], core)
    heads = prow.shape[1]
    xw = heads * MP

    conv, pay, cum = call(
        pre_kernel,
        (ids, doc_lengths),
        (rows, halo, taps, prow),
        (((tokens, width), BF16), ((xw + 2 * heads, MN), BF16), ((tokens, heads), F32)),
        (pltpu.VMEM((HALO + tokens, 2 * MP), F32),),
        name="pre",
    )
    kv_width = qkv.shape[1] - q_heads * HEAD_SIZE
    kv = jnp.stack(earlier(qkv[:, q_heads * HEAD_SIZE :], chips))
    pays = earlier(pay, chips)
    (intra,) = call(
        intra_kernel, (ids, doc_lengths), (rows, conv, cum, prow, pcol), (((tokens, xw), F32),),
        name="intra",
    )
    qw = q_heads * HEAD_SIZE
    a_own, a_other, a_sum = call(
        attention_kernel,
        (ids, doc_lengths, windows),
        (qkv, kv),
        (((half, qw), BF16), ((half, qw), BF16), ((1, qw), F32)),
        (
            pltpu.VMEM((tokens, qw), BF16),
            pltpu.VMEM((tokens, 128), F32),
            pltpu.VMEM((tokens, 128), F32),
            pltpu.VMEM((tokens, qw), F32),
        ),
        name="attention",
    )
    a_received = swap(a_other)
    m_own, m_other, m_sum = call(
        functools.partial(finish_kernel, chips - 1),
        (ids, doc_lengths),
        (*pays, intra, conv, cum, gain),
        (((half, xw), BF16), ((half, xw), BF16), ((1, xw), F32)),
        (pltpu.VMEM((tokens, xw), BF16),),
        name="finish",
    )
    m_received = swap(m_other)
    sums = lax.all_gather(jnp.concatenate([a_sum, m_sum], axis=1)[0], ("chip", "core"))
    sums = jnp.sum(sums.reshape(chips, PAIR, qw + xw), axis=0)
    return (
        join(core, a_own, a_received),
        join(core, m_own, m_received),
        sums[:, :qw].reshape(PAIR * qw),
        sums[:, qw:].reshape(PAIR * xw),
    )


def solution(mesh):
    seq, tensor = mesh.shape["seq"], mesh.shape["tensor"]
    paired = Mesh(mesh.devices.reshape(seq // PAIR, PAIR, tensor), ("chip", "core", "tensor"))
    tokens = ("chip", "core", "tensor")
    block = ("chip", "core")
    placed = (P(tokens, None),) * 7 + (P(None, "tensor"),) * 3 + (P("tensor"),) * 4 + (P(), P())
    return jax.shard_map(
        local,
        mesh=paired,
        in_specs=placed,
        out_specs=(P(block, "tensor"), P(block, "tensor"), P("tensor"), P("tensor")),
        check_vma=False,
    )
```

time: 187 us -> 97.4 us (0.52)
  blocking collectives: 55.4 us -> 11.8 us
  other arithmetic: 30.3 us -> 7.75 us
  between operations: 19 us -> 0.97 us
  Pallas kernels: 0 us -> 15 us
  matrix products: 12.8 us -> 0 us
  local copies, waits for them, and re-layouts: 16.8 us -> 10 us
  waiting for transfers between devices: 14.2 us -> 20.2 us
  starting transfers between devices: 36.3 us -> 30.9 us
    psum x1 -> x0, blocking collectives: 23.6 us -> none  [local(): lax.psum((jnp.sum(attention.astype(jnp.float32), axis=0), jnp.sum(mamba_o...]
    all_to_all x7 -> x2, starting transfers between devices: 31.4 us -> 10 us  [to_heads(): lax.all_to_all(packed, ('core', 'tensor'), split_axis=0, concat_axis=0, t...]
    all_gather x3 -> x1, blocking collectives: 31.8 us -> 11.8 us  [local(): lax.all_gather(jnp.concatenate([a_sum, m_sum], axis=1)[0], ('chip', 'core'))]
    ppermute x3 -> x9, starting transfers between devices: 4.82 us -> 20.9 us  [the longest x6 17.1 us: earlier(): lax.ppermute(block, 'chip', [(i, i + d) for i in range(chips - d)])]
    pallas_call x0 -> x4, Pallas kernels: none -> 15 us  [call(): pl.pallas_call(kernel, out_shape=[jax.ShapeDtypeStruct(shape, dtype) for...]
    dot_general x6 -> x0, matrix products: 12.8 us -> none  [the longest x1 4.35 us: compute(): jnp.einsum('gqts,sgd->gqtd', weights.astype(jnp.bfloat16), values_rank3,...]
    convert_element_type x12 -> x0, other arithmetic: 8.45 us -> none  [the longest x8 5.54 us: turn(): part[k].astype(own.dtype)]
    all_to_all x8 -> x0, local copies, waits for them, and re-layouts: 6.72 us -> none  [the longest x1 1.88 us: local(): lax.all_to_all(mamba_x, 'tensor', split_axis=1, concat_axis=0, tiled=True)]
  transfers between devices with their start and end apart: 11 -> 11, of which waited for: 4 -> 5; matrix products, arithmetic and copies ran while one was open for 20% -> 10% of each run, Pallas kernels for 0% -> 12%
where the time goes in v1:
time: 97.4 us; the launch traced here: 96.7 us
  starting transfers between devices  30.9 us (32%)
  waiting for transfers between devices  20.2 us (21%)
  Pallas kernels  15 us (15%)
  blocking collectives  11.8 us (12%)
  local copies, waits for them, and re-layouts  10 us (10%)
  other arithmetic  7.75 us (8%)
    all_to_all x2, waiting for transfers between devices, to_heads(): lax.all_to_all(packed, ('core', 'tensor'), split_axis=0, concat_axis=0, t...  18.9 us
    ppermute x6, starting transfers between devices, earlier(): lax.ppermute(block, 'chip', [(i, i + d) for i in range(chips - d)])  17.1 us
    pallas_call x4, Pallas kernels, call(): pl.pallas_call(kernel, out_shape=[jax.ShapeDtypeStruct(shape, dtype) for...  15 us
    all_gather x1, blocking collectives, local(): lax.all_gather(jnp.concatenate([a_sum, m_sum], axis=1)[0], ('chip', 'core'))  11.8 us
    all_to_all x2, starting transfers between devices, to_heads(): lax.all_to_all(packed, ('core', 'tensor'), split_axis=0, concat_axis=0, t...  10 us
    select_n x2, other arithmetic, join(): jnp.where(core == 0, jnp.concatenate([own, received], axis=1), jnp.concat...  3.7 us
    unnamed x44, local copies, waits for them, and re-layouts  3.53 us
    reshape x7, local copies, waits for them, and re-layouts, pack(): p.reshape(rows, tensor, PAIR, p.shape[1] // (tensor * PAIR))  3.45 us
  transfers between devices with their start and end apart: 11, of which 5 were waited for; matrix products, arithmetic and copies ran while one was open for 10% of the time, Pallas kernels for 12%

profile of v1, /device:TPU:0, one launch (start us, length us, event | category | flops | bytes accessed | tf_op | source)
XLA Modules:
  0.0 96.7 jit_solution(17559950883753196870)
XLA Ops:
  0.6 1.2 %reshape.51 = bf16[32,4,2,512]{3,2,1,0:T(2,128)(2,1)S(1)} reshape(bf16[32,4096]{1,0:T(8,128)(2,1)} %param.16) | data formatting | bytes 524288 | tf_op jit(solution)/shard_map/reshape | solution.py:306
  1.8 0.9 reshape.52
  2.7 0.9 reshape.53
  4.0 0.8 copy.36
  4.8 6.5 %all-to-all-start = ((bf16[8,32,768]{2,1,0:T(8,128)(2,1)}), bf16[8,32,768]{2,1,0:T(8,128)(2,1)S(1)}, u32[]{:S(2)}, u32[]{:S(2)}) async-start(bf16[8,32,768]{2,1,0:T(8,128)(2,1)} %bitcast.4), calls=%async_computation | async-start | bytes 786432 | tf_op jit(solution)/shard_map/all_to_all | solution.py:313
  12.8 0.9 copy.39
  13.8 9.5 %all-to-all-done = bf16[8,32,768]{2,1,0:T(8,128)(2,1)S(1)} async-done(((bf16[8,32,768]{2,1,0:T(8,128)(2,1)}), bf16[8,32,768]{2,1,0:T(8,128)(2,1)S(1)}, u32[]{:S(2)}, u32[]{:S(2)}) %all-to-all-start) | async-done | bytes 393248 | tf_op jit(solution)/shard_map/all_to_all | solution.py:313
  23.3 3.5 %all-to-all-start.1 = ((bf16[8,32,1296]{2,1,0:T(8,128)(2,1)}), bf16[8,32,1296]{2,1,0:T(8,128)(2,1)S(1)}, u32[]{:S(2)}, u32[]{:S(2)}) async-start(bf16[8,32,1296]{2,1,0:T(8,128)(2,1)} %bitcast.11), calls=%async_computation.1 | async-start | bytes 1441792 | tf_op jit(solution)/shard_map/all_to_all | solution.py:313
  27.6 3.4 %collective-permute-start = (bf16[256,256]{1,0:T(8,128)(2,1)S(1)}, bf16[256,256]{1,0:T(8,128)(2,1)S(1)}, u32[]{:S(2)}, u32[]{:S(2)}) collective-permute-start(bf16[256,256]{1,0:T(8,128)(2,1)S(1)} %slice.16), channel_id=1, source_target_pairs={{0,8},{8,16},{16,24},{1,9},{9,17},{17,25},{2,10},{10,18},{18,26},{... | collective-permute-start | bytes 393224 | tf_op jit(solution)/shard_map/ppermute | solution.py:319
  31.0 3.4 %collective-permute-start.1 = (bf16[256,256]{1,0:T(8,128)(2,1)S(1)}, bf16[256,256]{1,0:T(8,128)(2,1)S(1)}, u32[]{:S(2)}, u32[]{:S(2)}) collective-permute-start(bf16[256,256]{1,0:T(8,128)(2,1)S(1)} %slice.16), channel_id=1, source_target_pairs={{0,16},{8,24},{1,17},{9,25},{2,18},{10,26},{3,19},{11,27},{4,20},{... | collective-permute-start | bytes 393224 | tf_op jit(solution)/shard_map/ppermute | solution.py:319
  34.4 1.3 %collective-permute-start.2 = (bf16[256,256]{1,0:T(8,128)(2,1)S(1)}, bf16[256,256]{1,0:T(8,128)(2,1)S(1)}, u32[]{:S(2)}, u32[]{:S(2)}) collective-permute-start(bf16[256,256]{1,0:T(8,128)(2,1)S(1)} %slice.16), channel_id=1, source_target_pairs={{0,24},{1,25},{2,26},{3,27},{4,28},{5,29},{6,30},{7,31}} | collective-permute-start | bytes 393224 | tf_op jit(solution)/shard_map/ppermute | solution.py:319
  36.4 9.4 %all-to-all-done.1 = bf16[8,32,1296]{2,1,0:T(8,128)(2,1)S(1)} async-done(((bf16[8,32,1296]{2,1,0:T(8,128)(2,1)}), bf16[8,32,1296]{2,1,0:T(8,128)(2,1)S(1)}, u32[]{:S(2)}, u32[]{:S(2)}) %all-to-all-start.1) | async-done | bytes 663584 | tf_op jit(solution)/shard_map/all_to_all | solution.py:313
  45.8 3.4 %collective-permute-start.4 = (bf16[8,1280]{1,0:T(8,128)(2,1)S(1)}, bf16[8,1280]{1,0:T(8,128)(2,1)S(1)}, u32[]{:S(2)}, u32[]{:S(2)}) collective-permute-start(bf16[8,1280]{1,0:T(8,128)(2,1)S(1)} %slice.17), channel_id=1, source_target_pairs={{0,8},{8,16},{16,24},{1,9},{9,17},{17,25},{2,10},{10,18},{18,26},{... | collective-permute-start | bytes 61448 | tf_op jit(solution)/shard_map/ppermute | solution.py:359
  49.8 0.9 collective-permute-done.4.halo_ref
  51.2 4.2 %pre.1 = (bf16[256,1280]{1,0:T(8,128)(2,1)}, bf16[1056,128]{1,0:T(8,128)(2,1)}, f32[256,16]{1,0:T(8,128)}) custom-call(s32[3]{0:T(128)} %pad_add_fusion.ids, s32[3]{0:T(128)} %lengths.7, bf16[256,1296]{1,0:T(8,128)(2,1)} %bitcast.31, bf16[8,1280]{1,0:T(8,128)(2,1)} %copy-done.10, bf16[4,1280]{1,0:T(4,128)(2,1)} %pad_maximum_fusion.1.taps_ref, ...), custom_call_target="tpu_custom_call" | custom-call | tf_op jit(solution)/shard_map/pre/pallas_call | solution.py:294
  55.4 4.2 %collective-permute-start.5 = (bf16[1056,128]{1,0:T(8,128)(2,1)}, bf16[1056,128]{1,0:T(8,128)(2,1)S(1)}, u32[]{:S(2)}, u32[]{:S(2)}) collective-permute-start(bf16[1056,128]{1,0:T(8,128)(2,1)} %get-tuple-element.15), channel_id=1, source_target_pairs={{0,8},{8,16},{16,24},{1,9},{9,17},{17,25},{2,10},{10,18},{18,26},{... | collective-permute-start | bytes 811016 | tf_op jit(solution)/shard_map/ppermute | solution.py:319
  59.6 3.4 %collective-permute-start.6 = (bf16[1056,128]{1,0:T(8,128)(2,1)}, bf16[1056,128]{1,0:T(8,128)(2,1)S(1)}, u32[]{:S(2)}, u32[]{:S(2)}) collective-permute-start(bf16[1056,128]{1,0:T(8,128)(2,1)} %get-tuple-element.15), channel_id=1, source_target_pairs={{0,16},{8,24},{1,17},{9,25},{2,18},{10,26},{3,19},{11,27},{4,20},{... | collective-permute-start | bytes 811016 | tf_op jit(solution)/shard_map/ppermute | solution.py:319
  63.1 1.3 %collective-permute-start.7 = (bf16[1056,128]{1,0:T(8,128)(2,1)}, bf16[1056,128]{1,0:T(8,128)(2,1)S(1)}, u32[]{:S(2)}, u32[]{:S(2)}) collective-permute-start(bf16[1056,128]{1,0:T(8,128)(2,1)} %get-tuple-element.15), channel_id=1, source_target_pairs={{0,24},{1,25},{2,26},{3,27},{4,28},{5,29},{6,30},{7,31}} | collective-permute-start | bytes 811016 | tf_op jit(solution)/shard_map/ppermute | solution.py:319
  65.2 3.0 %attention.1 = (bf16[128,512]{1,0:T(8,128)(2,1)}, bf16[128,512]{1,0:T(8,128)(2,1)}, f32[1,512]{1,0:T(1,128)}) custom-call(s32[3]{0:T(128)} %pad_add_fusion.ids, s32[3]{0:T(128)} %lengths.7, s32[32]{0:T(128)} %windows.1, bf16[256,768]{1,0:T(8,128)(2,1)} %bitcast.34, bf16[3,256,256]{2,1,0:T(8,128)(2,1)} %pad_maximum_fusion.kv_ref), custom_call_target="tpu_custom_call" | custom-call | tf_op jit(solution)/shard_map/attention/pallas_call | solution.py:294
  69.8 1.8 %maximum_select_fusion.1 = bf16[128,1024]{1,0:T(8,128)(2,1)} fusion(bf16[128,512]{1,0:T(8,128)(2,1)S(1)} %collective-permute-done.3, bf16[128,512]{1,0:T(8,128)(2,1)} %get-tuple-element.13, pred[]{:T(512)S(6)} %eq.4), kind=kLoop, calls=%fused_computation.4 | loop fusion | flops 1179648 | bytes 524289 | tf_op jit(solution)/shard_map/jit(_where)/select_n | solution.py:334
  71.6 4.1 %intra.1.refs_3_ = f32[256,1024]{1,0:T(8,128)} custom-call(s32[3]{0:T(128)} %pad_add_fusion.ids, s32[3]{0:T(128)} %lengths.7, bf16[256,1296]{1,0:T(8,128)(2,1)} %bitcast.32, bf16[256,1280]{1,0:T(8,128)(2,1)} %get-tuple-element.16.conv_ref.refs_4_, f32[256,16]{1,0:T(8,128)} %get-tuple-element.17.cum_ref.refs_5_, f32[3,16]{1,0:T(4,128)} %constant_dynamic-slice_fusion.prow_ref, ...), custom_call_target="tpu_custom_call" | custom-call | tf_op jit(solution)/shard_map/intra/pallas_call | solution.py:294
  76.5 3.8 %finish.1 = (bf16[128,1024]{1,0:T(8,128)(2,1)}, bf16[128,1024]{1,0:T(8,128)(2,1)}, f32[1,1024]{1,0:T(1,128)}) custom-call(s32[3]{0:T(128)} %pad_add_fusion.ids, s32[3]{0:T(128)} %lengths.7, bf16[1056,128]{1,0:T(8,128)(2,1)} %copy-done.4, bf16[1056,128]{1,0:T(8,128)(2,1)} %copy-done.5, bf16[1056,128]{1,0:T(8,128)(2,1)} %copy-done.6, ...), custom_call_target="tpu_custom_call" | custom-call | tf_op jit(solution)/shard_map/finish/pallas_call | solution.py:294
  81.0 11.8 %all-gather = f32[8,1,1536]{2,1,0:T(1,128)S(1)} all-gather(f32[1,1,1536]{2,1,0:T(1,128)S(1)} %maximum_bitcast_fusion.2), channel_id=1, replica_groups=mesh['chip'=4,'core'=2,'tensor'=4] {'chip','core'}, dimensions={0}, use_global_device_ids=true | all-gather | bytes 55296 | tf_op jit(solution)/shard_map/all_gather | solution.py:407
  94.7 1.9 %maximum_select_fusion = bf16[128,2048]{1,0:T(8,128)(2,1)} fusion(bf16[128,1024]{1,0:T(8,128)(2,1)S(1)} %collective-permute-done.8, bf16[128,1024]{1,0:T(8,128)(2,1)} %get-tuple-element.18, pred[]{:T(512)S(6)} %eq.4), kind=kLoop, calls=%fused_computation.1 | loop fusion | flops 2359296 | bytes 1048577 | tf_op jit(solution)/shard_map/jit(_where)/select_n | solution.py:334
  (74 shorter events, 10.3 us)
Async XLA Ops:
  0.6 26.3 %copy-start = (bf16[4,2048]{1,0:T(4,128)(2,1)S(1)}, bf16[4,2048]{1,0:T(4,128)(2,1)}, u32[]{:S(2)}) copy-start(bf16[4,2048]{1,0:T(4,128)(2,1)} %param.23) | copy-start | bytes 49156
  3.6 7.7 %copy-start.3 = (bf16[32,8192]{1,0:T(8,128)(2,1)S(1)}, bf16[32,8192]{1,0:T(8,128)(2,1)}, u32[]{:S(2)}) copy-start(bf16[32,8192]{1,0:T(8,128)(2,1)} %param.19) | copy-start | bytes 1572868
  4.8 6.9 %copy-start.11 = (bf16[32,128]{1,0:T(8,128)(2,1)S(1)}, bf16[32,128]{1,0:T(8,128)(2,1)}, u32[]{:S(2)}) copy-start(bf16[32,128]{1,0:T(8,128)(2,1)} %param.22) | copy-start | bytes 24580
  4.8 7.1 %copy-start.7 = (bf16[32,1024]{1,0:T(8,128)(2,1)S(1)}, bf16[32,1024]{1,0:T(8,128)(2,1)}, u32[]{:S(2)}) copy-start(bf16[32,1024]{1,0:T(8,128)(2,1)} %param.20) | copy-start | bytes 196612
  4.8 7.2 %copy-start.8 = (bf16[32,1024]{1,0:T(8,128)(2,1)S(1)}, bf16[32,1024]{1,0:T(8,128)(2,1)}, u32[]{:S(2)}) copy-start(bf16[32,1024]{1,0:T(8,128)(2,1)} %param.21) | copy-start | bytes 196612
  4.8 18.5 %all-to-all-start = ((bf16[8,32,768]{2,1,0:T(8,128)(2,1)}), bf16[8,32,768]{2,1,0:T(8,128)(2,1)S(1)}, u32[]{:S(2)}, u32[]{:S(2)}) async-start(bf16[8,32,768]{2,1,0:T(8,128)(2,1)} %bitcast.4), calls=%async_computation | async-start | bytes 786432 | tf_op jit(solution)/shard_map/all_to_all | solution.py:313
  13.7 13.1 %copy-start.17 = (bf16[4,256]{1,0:T(4,128)(2,1)S(1)}, bf16[4,256]{1,0:T(4,128)(2,1)}, u32[]{:S(2)}) copy-start(bf16[4,256]{1,0:T(4,128)(2,1)} %param.25) | copy-start | bytes 6148
  13.8 13.1 %copy-start.18 = (bf16[4,256]{1,0:T(4,128)(2,1)S(1)}, bf16[4,256]{1,0:T(4,128)(2,1)}, u32[]{:S(2)}) copy-start(bf16[4,256]{1,0:T(4,128)(2,1)} %param.24) | copy-start | bytes 6148
  13.8 13.1 %copy-start.14 = (f32[32]{0:T(128)S(1)}, f32[32]{0:T(128)}, u32[]{:S(2)}) copy-start(f32[32]{0:T(128)} %param.28) | copy-start | bytes 388
  13.8 13.1 %copy-start.15 = (f32[32]{0:T(128)S(1)}, f32[32]{0:T(128)}, u32[]{:S(2)}) copy-start(f32[32]{0:T(128)} %param.27) | copy-start | bytes 388
  13.8 13.1 %copy-start.16 = (f32[32]{0:T(128)S(1)}, f32[32]{0:T(128)}, u32[]{:S(2)}) copy-start(f32[32]{0:T(128)} %param.26) | copy-start | bytes 388
  23.3 32.1 %copy-start.2 = (bf16[8,32,768]{2,1,0:T(8,128)(2,1)}, bf16[8,32,768]{2,1,0:T(8,128)(2,1)S(1)}, u32[]{:S(2)}) copy-start(bf16[8,32,768]{2,1,0:T(8,128)(2,1)S(1)} %all-to-all-done) | copy-start | bytes 1179652
  23.3 22.5 %all-to-all-start.1 = ((bf16[8,32,1296]{2,1,0:T(8,128)(2,1)}), bf16[8,32,1296]{2,1,0:T(8,128)(2,1)S(1)}, u32[]{:S(2)}, u32[]{:S(2)}) async-start(bf16[8,32,1296]{2,1,0:T(8,128)(2,1)} %bitcast.11), calls=%async_computation.1 | async-start | bytes 1441792 | tf_op jit(solution)/shard_map/all_to_all | solution.py:313
  27.6 35.5 %collective-permute-start = (bf16[256,256]{1,0:T(8,128)(2,1)S(1)}, bf16[256,256]{1,0:T(8,128)(2,1)S(1)}, u32[]{:S(2)}, u32[]{:S(2)}) collective-permute-start(bf16[256,256]{1,0:T(8,128)(2,1)S(1)} %slice.16), channel_id=1, source_target_pairs={{0,8},{8,16},{16,24},{1,9},{9,17},{17,25},{2,10},{10,18},{18,26},{... | collective-permute-start | bytes 393224 | tf_op jit(solution)/shard_map/ppermute | solution.py:319
  31.0 33.4 %collective-permute-start.1 = (bf16[256,256]{1,0:T(8,128)(2,1)S(1)}, bf16[256,256]{1,0:T(8,128)(2,1)S(1)}, u32[]{:S(2)}, u32[]{:S(2)}) collective-permute-start(bf16[256,256]{1,0:T(8,128)(2,1)S(1)} %slice.16), channel_id=1, source_target_pairs={{0,16},{8,24},{1,17},{9,25},{2,18},{10,26},{3,19},{11,27},{4,20},{... | collective-permute-start | bytes 393224 | tf_op jit(solution)/shard_map/ppermute | solution.py:319
  34.4 30.0 %collective-permute-start.2 = (bf16[256,256]{1,0:T(8,128)(2,1)S(1)}, bf16[256,256]{1,0:T(8,128)(2,1)S(1)}, u32[]{:S(2)}, u32[]{:S(2)}) collective-permute-start(bf16[256,256]{1,0:T(8,128)(2,1)S(1)} %slice.16), channel_id=1, source_target_pairs={{0,24},{1,25},{2,26},{3,27},{4,28},{5,29},{6,30},{7,31}} | collective-permute-start | bytes 393224 | tf_op jit(solution)/shard_map/ppermute | solution.py:319
  45.8 4.9 %collective-permute-start.4 = (bf16[8,1280]{1,0:T(8,128)(2,1)S(1)}, bf16[8,1280]{1,0:T(8,128)(2,1)S(1)}, u32[]{:S(2)}, u32[]{:S(2)}) collective-permute-start(bf16[8,1280]{1,0:T(8,128)(2,1)S(1)} %slice.17), channel_id=1, source_target_pairs={{0,8},{8,16},{16,24},{1,9},{9,17},{17,25},{2,10},{10,18},{18,26},{... | collective-permute-start | bytes 61448 | tf_op jit(solution)/shard_map/ppermute | solution.py:359
  49.8 18.5 %copy-start.9 = (f32[3,16]{1,0:T(4,128)S(1)}, f32[3,16]{1,0:T(4,128)}, u32[]{:S(2)}) copy-start(f32[3,16]{1,0:T(4,128)} %constant_dynamic-slice_fusion.prow_ref) | copy-start | bytes 580
  49.8 19.2 %copy-start.12 = (f32[2048]{0:T(1024)S(1)}, f32[2048]{0:T(1024)}, u32[]{:S(2)}) copy-start(f32[2048]{0:T(1024)} %param.29) | copy-start | bytes 24580
  55.4 20.2 %collective-permute-start.5 = (bf16[1056,128]{1,0:T(8,128)(2,1)}, bf16[1056,128]{1,0:T(8,128)(2,1)S(1)}, u32[]{:S(2)}, u32[]{:S(2)}) collective-permute-start(bf16[1056,128]{1,0:T(8,128)(2,1)} %get-tuple-element.15), channel_id=1, source_target_pairs={{0,8},{8,16},{16,24},{1,9},{9,17},{17,25},{2,10},{10,18},{18,26},{... | collective-permute-start | bytes 811016 | tf_op jit(solution)/shard_map/ppermute | solution.py:319
  59.6 16.0 %collective-permute-start.6 = (bf16[1056,128]{1,0:T(8,128)(2,1)}, bf16[1056,128]{1,0:T(8,128)(2,1)S(1)}, u32[]{:S(2)}, u32[]{:S(2)}) collective-permute-start(bf16[1056,128]{1,0:T(8,128)(2,1)} %get-tuple-element.15), channel_id=1, source_target_pairs={{0,16},{8,24},{1,17},{9,25},{2,18},{10,26},{3,19},{11,27},{4,20},{... | collective-permute-start | bytes 811016 | tf_op jit(solution)/shard_map/ppermute | solution.py:319
  63.1 12.6 %collective-permute-start.7 = (bf16[1056,128]{1,0:T(8,128)(2,1)}, bf16[1056,128]{1,0:T(8,128)(2,1)S(1)}, u32[]{:S(2)}, u32[]{:S(2)}) collective-permute-start(bf16[1056,128]{1,0:T(8,128)(2,1)} %get-tuple-element.15), channel_id=1, source_target_pairs={{0,24},{1,25},{2,26},{3,27},{4,28},{5,29},{6,30},{7,31}} | collective-permute-start | bytes 811016 | tf_op jit(solution)/shard_map/ppermute | solution.py:319
  68.3 1.6 %collective-permute-start.3 = (bf16[128,512]{1,0:T(8,128)(2,1)}, bf16[128,512]{1,0:T(8,128)(2,1)S(1)}, u32[]{:S(2)}, u32[]{:S(2)}) collective-permute-start(bf16[128,512]{1,0:T(8,128)(2,1)} %get-tuple-element.14), channel_id=1, source_target_pairs={{0,4},{4,0},{1,5},{5,1},{2,6},{6,2},{3,7},{7,3},{8,12},{12,8},{9,1... | collective-permute-start | bytes 393224 | tf_op jit(solution)/shard_map/ppermute | solution.py:330
  92.9 1.8 %collective-permute-start.8 = (bf16[128,1024]{1,0:T(8,128)(2,1)}, bf16[128,1024]{1,0:T(8,128)(2,1)S(1)}, u32[]{:S(2)}, u32[]{:S(2)}) collective-permute-start(bf16[128,1024]{1,0:T(8,128)(2,1)} %get-tuple-element.19), channel_id=1, source_target_pairs={{0,4},{4,0},{1,5},{5,1},{2,6},{6,2},{3,7},{7,3},{8,12},{12,8},{9,1... | collective-permute-start | bytes 786440 | tf_op jit(solution)/shard_map/ppermute | solution.py:330
  (6 other events, 11.6 us)
